TPU v7x, 128 devices: a whole 4x4x4 slice. The times are simulated.
128 devices in a mesh: row: 8 (over y, core), col: 16 (over z, x).
Axes of the slice: x: 4, y: 4, z: 4, core: 2. Of those that a mesh axis runs over, the one named last changes fastest.
Arguments:
- dealing: int32 [8, 16], P('row'), may hold values from 0 to 15, each once within a row
- residual: bfloat16 [8192, 3072], P('row', 'col'), may hold values from -6 to 6
- queries: bfloat16 [8192, 3072], P('row', 'col'), may hold values from -6 to 6
- draft_keys: bfloat16 [8192, 3072], P('row', 'col'), may hold values from -6 to 6
- draft_values: bfloat16 [8192, 3072], P('row', 'col'), may hold values from -6 to 6
- cache_keys: bfloat16 [128, 1536, 3072], P(('row', 'col')), may hold values from -6 to 6
- cache_values: bfloat16 [128, 1536, 3072], P(('row', 'col')), may hold values from -6 to 6
- cache_lengths: int32 [128], P(('row', 'col')), may hold values from 97 to 1536, as said below
- parents: int32 [128, 64], P(('row', 'col')), may hold values from -1 to 62, as said below
- draft_counts: int32 [128], P(('row', 'col')), may hold values from 32 to 64, as said below
- accepted: int32 [128, 8], P(('row', 'col')), may hold values from -1 to 28, as said below
- out_weight: bfloat16 [3072, 3072], P('row', 'col'), may hold values from -0.109375 to 0.109375
- norm_gain: bfloat16 [3072], P('col'), may hold values from 0.099609375 to 1.8984375
- gate_weight: bfloat16 [3072, 8192], P('row', 'col'), may hold values from -0.109375 to 0.109375
- up_weight: bfloat16 [3072, 8192], P('row', 'col'), may hold values from -0.109375 to 0.109375
- down_weight: bfloat16 [8192, 3072], P('col', 'row'), may hold values from -0.09375 to 0.09375
Outputs:
- layer_out: bfloat16 [8192, 3072], P('row', 'col')
- new_keys: bfloat16 [128, 8, 3072], P(('row', 'col'))
- new_values: bfloat16 [128, 8, 3072], P(('row', 'col'))
Inputs may be any that keep to these rules, and one draw needn't show every extreme that they name: Each row of dealing names every index along col once. `cache_lengths`: the largest is 1536 in every draw. parents[s, 0] = -1, and for i >= 1, i - 4 <= parents[s, i] < i. `draft_counts`: the largest is 64 in every draw. `accepted`: each row lists draft tokens from the root 0 downward, each the child under parents of the one before and below the slot's draft count, then -1; some row fills all 8 entries, and the largest entry is 28 in every draw.
All inputs are finite; a program needn't handle non-finite values.
Results may differ from a plain program's by a relative error of at most 0.017.
Values may be sent and summed in bfloat16 or wider, within the bound.
A program may use at most 128 MiB of HBM per device.

v0:
```python
import math
import jax
import jax.numpy as jnp
from jax import lax
from jax.sharding import PartitionSpec as P

D = 3072
HEADS = 32
HEAD_DIM = 96


def ancestry(parent_row):
    count_all = parent_row.shape[0]
    token_index = jnp.arange(count_all, dtype=jnp.int32)
    linked = jnp.logical_or(
        parent_row[:, None] == token_index[None, :], token_index[:, None] == token_index[None, :]
    )
    ancestors = linked.astype(jnp.float32)
    for sweep in range(max(1, (count_all - 1).bit_length())):
        ancestors = jnp.minimum(jnp.dot(ancestors, ancestors, precision=lax.Precision.HIGHEST), 1.0)
    return ancestors


def rotate(value_rows, position):
    row_count = value_rows.shape[0]
    half_dim = HEAD_DIM // 2
    shaped = value_rows.astype(jnp.float32).reshape(row_count, HEADS, HEAD_DIM)
    frequency = jnp.power(10000.0, -jnp.arange(half_dim, dtype=jnp.float32) * (2.0 / HEAD_DIM))
    angles = position[:, None] * frequency[None, :]
    cosine = jnp.cos(angles)[:, None, :]
    sine_part = jnp.sin(angles)[:, None, :]
    front_half = shaped[..., :half_dim]
    back_half = shaped[..., half_dim:]
    turned = jnp.concatenate(
        [front_half * cosine - back_half * sine_part, back_half * cosine + front_half * sine_part],
        axis=-1,
    )
    return turned.reshape(row_count, HEADS * HEAD_DIM).astype(jnp.bfloat16)


def fold_block(state_now, q_heads, key_block, value_block, allowed):
    running_max, row_totals, accumulator = state_now
    score_scale = 1.0 / math.sqrt(HEAD_DIM)
    key_heads = key_block.reshape(key_block.shape[0], HEADS, HEAD_DIM)
    value_heads = value_block.reshape(value_block.shape[0], HEADS, HEAD_DIM)
    scores = (
        jnp.einsum("qhd,khd->hqk", q_heads, key_heads, preferred_element_type=jnp.float32)
        * score_scale
    )
    scores = jnp.where(allowed[None], scores, -jnp.inf)
    new_max = jnp.maximum(running_max, jnp.max(scores, axis=2))
    rescale = jnp.exp(running_max - new_max)
    weights = jnp.exp(scores - new_max[:, :, None])
    row_totals = row_totals * rescale + jnp.sum(weights, axis=2)
    mixed_rows = jnp.einsum(
        "hqk,khd->qhd",
        weights.astype(jnp.bfloat16),
        value_heads,
        preferred_element_type=jnp.float32,
    )
    accumulator = accumulator * rescale.T[:, :, None] + mixed_rows
    return (new_max, row_totals, accumulator)


def verify_slot(
    query_rows, key_rows, value_rows, cache_k, cache_v, length, parent_row, live_count, path_row
):
    draft_rows = query_rows.shape[0]
    width = query_rows.shape[1]
    ancestors = ancestry(parent_row)
    tree_depth = jnp.sum(ancestors, axis=1) - 1.0
    position = length.astype(jnp.float32) + tree_depth
    q_rot = rotate(query_rows, position)
    k_rot = rotate(key_rows, position)
    q_heads = q_rot.reshape(draft_rows, HEADS, HEAD_DIM)
    cache_rows = cache_k.shape[0]
    block_rows = min(512, cache_rows)

    def cache_step(block_step, state_now):
        block_start = block_step * block_rows
        key_block = lax.dynamic_slice_in_dim(cache_k, block_start, block_rows, 0)
        value_block = lax.dynamic_slice_in_dim(cache_v, block_start, block_rows, 0)
        live_keys = block_start + jnp.arange(block_rows, dtype=jnp.int32) < length
        allowed = jnp.broadcast_to(live_keys[None, :], (draft_rows, block_rows))
        return fold_block(state_now, q_heads, key_block, value_block, allowed)

    initial = (
        jnp.full((HEADS, draft_rows), -jnp.inf, jnp.float32),
        jnp.zeros((HEADS, draft_rows), jnp.float32),
        jnp.zeros((draft_rows, HEADS, HEAD_DIM), jnp.float32),
    )
    block_total = cache_rows // block_rows
    state_now = lax.fori_loop(0, block_total, cache_step, initial)
    token_index = jnp.arange(draft_rows, dtype=jnp.int32)
    allowed = jnp.logical_and(ancestors > 0.5, token_index[None, :] < live_count)
    running_max, row_totals, accumulator = fold_block(
        state_now, q_heads, k_rot, value_rows, allowed
    )
    attended = (
        (accumulator / row_totals.T[:, :, None]).reshape(draft_rows, width).astype(jnp.bfloat16)
    )
    selector = (path_row[:, None] == token_index[None, :]).astype(jnp.bfloat16)
    new_keys = jnp.dot(selector, k_rot, preferred_element_type=jnp.float32).astype(jnp.bfloat16)
    new_values = jnp.dot(selector, value_rows, preferred_element_type=jnp.float32).astype(
        jnp.bfloat16
    )
    return (attended, new_keys, new_values)


def body(
    dealing,
    residual,
    queries,
    draft_keys,
    draft_values,
    cache_keys,
    cache_values,
    cache_lengths,
    parents,
    draft_counts,
    accepted,
    out_weight,
    norm_gain,
    gate_weight,
    up_weight,
    down_weight,
):
    columns = lax.axis_size("col")
    dealt_order = dealing[0]
    rows_here = residual.shape[0]
    draft_rows = rows_here // columns

    def to_slots(block_rows):
        shaped = block_rows.reshape(columns, draft_rows, block_rows.shape[1])
        return jnp.take(shaped, dealt_order, axis=0).reshape(rows_here, block_rows.shape[1])

    mine_q, mine_k, mine_v = (
        lax.all_to_all(to_slots(queries), "col", split_axis=0, concat_axis=1, tiled=True),
        lax.all_to_all(to_slots(draft_keys), "col", split_axis=0, concat_axis=1, tiled=True),
        lax.all_to_all(to_slots(draft_values), "col", split_axis=0, concat_axis=1, tiled=True),
    )
    attended, new_keys, new_values = verify_slot(
        mine_q,
        mine_k,
        mine_v,
        cache_keys[0],
        cache_values[0],
        cache_lengths[0],
        parents[0],
        draft_counts[0],
        accepted[0],
    )
    weight_cols = lax.all_gather(out_weight, "row", axis=0, tiled=True)
    projected = jnp.dot(
        lax.all_gather(attended, "col", axis=0, tiled=True),
        weight_cols,
        preferred_element_type=jnp.float32,
    )
    inverse = jnp.argsort(dealt_order)
    projected = jnp.take(
        projected.reshape(columns, draft_rows, projected.shape[1]), inverse, axis=0
    ).reshape(rows_here, projected.shape[1])
    stream_full = residual.astype(jnp.float32) + projected
    stream = stream_full.astype(jnp.bfloat16)
    stream_wide = lax.optimization_barrier(stream).astype(jnp.float32)
    local_sums = jnp.sum(stream_wide * stream_wide, axis=1)
    row_totals = lax.psum(local_sums, "col")
    factor = lax.rsqrt(row_totals / D + 1e-05)[:, None]
    normed = (stream_wide * factor * norm_gain.astype(jnp.float32)[None, :]).astype(jnp.bfloat16)
    gathered = lax.all_gather(normed, "col", axis=1, tiled=True)
    gate_next = jnp.dot(
        gathered,
        lax.all_gather(gate_weight, "row", axis=0, tiled=True),
        preferred_element_type=jnp.float32,
    )
    up_next = jnp.dot(
        gathered,
        lax.all_gather(up_weight, "row", axis=0, tiled=True),
        preferred_element_type=jnp.float32,
    )
    hidden = (jax.nn.silu(gate_next) * up_next).astype(jnp.bfloat16)
    partial_terms = jnp.dot(
        hidden,
        lax.all_gather(down_weight, "row", axis=1, tiled=True),
        preferred_element_type=jnp.float32,
    )
    summed = lax.psum_scatter(
        partial_terms.astype(jnp.bfloat16), "col", scatter_dimension=1, tiled=True
    ).astype(jnp.float32)
    layer_out = (stream_wide + summed).astype(jnp.bfloat16)
    return (layer_out, new_keys[None], new_values[None])


def solution(mesh):
    placed = (
        P("row", None),
        P("row", "col"),
        P("row", "col"),
        P("row", "col"),
        P("row", "col"),
        P(("row", "col"), None, None),
        P(("row", "col"), None, None),
        P(("row", "col")),
        P(("row", "col"), None),
        P(("row", "col")),
        P(("row", "col"), None),
        P("row", "col"),
        P("col"),
        P("row", "col"),
        P("row", "col"),
        P("col", "row"),
    )
    return jax.shard_map(
        body,
        mesh=mesh,
        in_specs=placed,
        out_specs=(P("row", "col"), P(("row", "col"), None, None), P(("row", "col"), None, None)),
        check_vma=False,
    )
```

profile of v0, /device:TPU:0, one launch (start us, length us, event | category | flops | bytes accessed | tf_op | source)
XLA Modules:
  0.0 458.0 jit_solution(15680085825392630706)
XLA Ops:
  14.3 8.0 %all-to-all-start.1 = ((bf16[16,64,192]{2,1,0:T(8,128)(2,1)}), bf16[16,64,192]{2,1,0:T(8,128)(2,1)S(1)}, u32[]{:S(2)}, u32[]{:S(2)}) async-start(bf16[16,64,192]{2,1,0:T(8,128)(2,1)} %get-tuple-element.212), calls=%async_computation.1 | async-start | bytes 1048576 | tf_op jit(solution)/shard_map/all_to_all | solution.py:139
  25.6 12.8 %copy.22 = bf16[1,1536,3072]{1,2,0:T(8,128)(2,1)} copy(bf16[1,1536,3072]{2,1,0:T(8,128)(2,1)} %param.25) | data formatting | bytes 18874368 | tf_op args[5]
  38.4 12.6 %copy.27 = bf16[1,1536,3072]{1,2,0:T(8,128)(2,1)} copy(bf16[1,1536,3072]{2,1,0:T(8,128)(2,1)} %param.26) | data formatting | bytes 18874368 | tf_op args[6]
  51.2 7.4 %all-to-all-start = ((bf16[16,64,192]{2,1,0:T(8,128)(2,1)}), bf16[16,64,192]{2,1,0:T(8,128)(2,1)}, u32[]{:S(2)}, u32[]{:S(2)}) async-start(bf16[16,64,192]{2,1,0:T(8,128)(2,1)} %get-tuple-element.213), calls=%async_computation | async-start | bytes 1048576 | tf_op jit(solution)/shard_map/all_to_all | solution.py:138
  60.0 9.6 %all-to-all-done = bf16[16,64,192]{2,1,0:T(8,128)(2,1)} async-done(((bf16[16,64,192]{2,1,0:T(8,128)(2,1)}), bf16[16,64,192]{2,1,0:T(8,128)(2,1)}, u32[]{:S(2)}, u32[]{:S(2)}) %all-to-all-start) | async-done | bytes 393248 | tf_op jit(solution)/shard_map/all_to_all | solution.py:138
  69.5 4.2 all-to-all-start.2
  82.6 40.6 %while.18 = (s32[]{:T(128)}, f32[32,64]{1,0:T(8,128)S(1)}, f32[32,64]{1,0:T(8,128)S(1)}, f32[64,32,96]{2,0,1:T(8,128)}, s32[]{:T(128)}, /*index=5*/bf16[1536,307...) while((s32[]{:T(128)}, f32[32,64]{1,0:T(8,128)S(1)}, ...), condition=%wide.region_5.7_spmd.clone, body=%wide.region_2.6_spmd.clone.sunk | while | flops 414790656 | bytes 51906808 | solution.py:93
  83.3 3.3 constant_dynamic-slice_fusion.3
  89.5 3.4 fusion.84
  96.2 3.3 constant_dynamic-slice_fusion.3
  102.3 3.4 fusion.84
  105.8 3.6 fusion.86
  110.0 3.3 constant_dynamic-slice_fusion.3
  116.2 3.4 fusion.84
  119.6 3.6 fusion.86
  132.4 60.7 %all-gather.7.cloned.1.call-done = bf16[1024,3072]{1,0:T(8,128)(2,1)} async-done(((bf16[64,3072]{1,0:T(8,128)(2,1)}), bf16[1024,3072]{1,0:T(8,128)(2,1)}) %all-gather.7.cloned.1.call-update) | async-done | bytes 6291472 | tf_op jit(solution)/shard_map/all_gather | solution.py:155
  193.1 4.9 %fusion.45 = f32[1024,192]{1,0:T(8,128)S(1)} fusion(bf16[1024,3072]{1,0:T(8,128)(2,1)} %all-gather.7.cloned.1.call-done, bf16[3072,192]{0,1:T(8,128)(2,1)} %all-gather.9.cloned.1.call-done), kind=kOutput, calls=%fused_computation.98 | convolution fusion | flops 1207959552 | bytes 8257536 | tf_op jit(solution)/shard_map/dot_general | solution.py:154
  199.3 38.4 %psum.7 = f32[1024]{0:T(1024)S(1)} all-reduce(f32[1024]{0:T(1024)S(1)} %fusion.27), channel_id=1, replica_groups=mesh['row'=8,'col'=16] {'col'}, use_global_device_ids=true, to_apply=%region_9.11 | all-reduce | flops 1024 | bytes 8192 | tf_op jit(solution)/shard_map/psum | solution.py:167
  239.8 56.6 %all-gather.11.cloned.1.call-done = bf16[1024,3072]{0,1:T(8,128)(2,1)} async-done(((bf16[1024,192]{0,1:T(8,128)(2,1)}), bf16[1024,3072]{0,1:T(8,128)(2,1)}) %all-gather.11.cloned.1.call-update) | async-done | bytes 6291472 | tf_op jit(solution)/shard_map/all_gather | solution.py:170
  296.4 6.5 %fusion.46 = f32[1024,512]{1,0:T(8,128)S(1)} fusion(bf16[1024,3072]{0,1:T(8,128)(2,1)} %all-gather.11.cloned.1.call-done, bf16[3072,512]{1,0:T(8,128)(2,1)} %all-gather.13.cloned.1.call-done), kind=kOutput, calls=%fused_computation.99 | convolution fusion | flops 3221225472 | bytes 11534336 | tf_op jit(solution)/shard_map/dot_general | solution.py:171
  302.9 22.3 %all-gather.17.cloned.1.call-done = bf16[512,3072]{1,0:T(8,128)(2,1)} async-done(((bf16[512,384]{1,0:T(8,128)(2,1)}), bf16[512,3072]{1,0:T(8,128)(2,1)}) %all-gather.17.cloned.1.call-update) | async-done | bytes 3145744 | tf_op jit(solution)/shard_map/all_gather | solution.py:184
  325.2 29.4 %all-gather.15.cloned.1.call-done = bf16[3072,512]{1,0:T(8,128)(2,1)} async-done(((bf16[384,512]{1,0:T(8,128)(2,1)}), bf16[3072,512]{1,0:T(8,128)(2,1)}) %all-gather.15.cloned.1.call-update) | async-done | bytes 3145744 | tf_op jit(solution)/shard_map/all_gather | solution.py:178
  354.6 12.8 %convolution_convert_fusion = bf16[1024,3072]{0,1:T(8,128)(2,1)} fusion(bf16[512,3072]{1,0:T(8,128)(2,1)} %all-gather.17.cloned.1.call-done, f32[1024,512]{1,0:T(8,128)S(1)} %fusion.46, bf16[1024,3072]{0,1:T(8,128)(2,1)} %all-gather.11.cloned.1.call-done, bf16[3072,512]{1,0:T(8,128)(2,1)} %all-gather.15.cloned.1.call-done), kind=kOutput, calls=%fused_computation.28 | convolution fusion | flops 6448742400 | bytes 20971520 | tf_op jit(solution)/shard_map/dot_general | solution.py:182
  371.8 77.5 %reduce-scatter.2.cloned.1.call-done = bf16[1024,192]{0,1:T(8,128)(2,1)} async-done(((bf16[1024,3072]{0,1:T(8,128)(2,1)}), bf16[1024,192]{0,1:T(8,128)(2,1)}) %reduce-scatter.2.cloned.1.call-update) | async-done | bytes 393232 | tf_op jit(solution)/shard_map/reduce_scatter | solution.py:187
  (126 shorter events, 51.0 us)
Async XLA Ops:
  7.2 5.0 %copy-start.3 = (bf16[1024,192]{0,1:T(8,128)(2,1)S(1)}, bf16[1024,192]{0,1:T(8,128)(2,1)}, u32[]{:S(2)}) copy-start(bf16[1024,192]{0,1:T(8,128)(2,1)} %param.22) | copy-start | bytes 1179652
  11.0 12.1 %copy-start.6 = (s32[1,64]{1,0:T(1,128)S(1)}, s32[1,64]{1,0:T(1,128)}, u32[]{:S(2)}) copy-start(s32[1,64]{1,0:T(1,128)} %param.28) | copy-start | bytes 772
  14.3 36.9 %all-to-all-start.1 = ((bf16[16,64,192]{2,1,0:T(8,128)(2,1)}), bf16[16,64,192]{2,1,0:T(8,128)(2,1)S(1)}, u32[]{:S(2)}, u32[]{:S(2)}) async-start(bf16[16,64,192]{2,1,0:T(8,128)(2,1)} %get-tuple-element.212), calls=%async_computation.1 | async-start | bytes 1048576 | tf_op jit(solution)/shard_map/all_to_all | solution.py:139
  22.3 110.1 %all-gather.9.cloned.1.call-start = ((), (), s32[]{:S(2)}) async-start(), calls=%async_computation.5 | async-start | bytes 1327104 | tf_op jit(solution)/shard_map/all_gather | solution.py:153
  51.2 18.3 %all-to-all-start = ((bf16[16,64,192]{2,1,0:T(8,128)(2,1)}), bf16[16,64,192]{2,1,0:T(8,128)(2,1)}, u32[]{:S(2)}, u32[]{:S(2)}) async-start(bf16[16,64,192]{2,1,0:T(8,128)(2,1)} %get-tuple-element.213), calls=%async_computation | async-start | bytes 1048576 | tf_op jit(solution)/shard_map/all_to_all | solution.py:138
  69.5 53.7 %all-to-all-start.2 = ((bf16[16,64,192]{2,1,0:T(8,128)(2,1)}), bf16[16,64,192]{2,1,0:T(8,128)(2,1)}, u32[]{:S(2)}, u32[]{:S(2)}) async-start(bf16[16,64,192]{2,1,0:T(8,128)(2,1)} %get-tuple-element.211), calls=%async_computation.2 | async-start | bytes 1048576 | tf_op jit(solution)/shard_map/all_to_all | solution.py:140
  73.8 119.4 %all-gather.7.cloned.1.call-start = ((), (), s32[]{:S(2)}) async-start(), calls=%async_computation.4 | async-start | bytes 6684672 | tf_op jit(solution)/shard_map/all_gather | solution.py:155
  83.3 3.3 copy-start.1
  89.5 3.4 copy-start
  96.2 3.3 copy-start.1
  102.3 3.4 copy-start
  110.0 3.3 copy-start.1
  116.2 3.4 copy-start
  123.2 3.6 copy-start.9
  126.8 4.2 copy-start.7
  126.8 5.6 %copy-start.8 = (bf16[192]{0:T(256)(128)(2,1)S(1)}, bf16[192]{0:T(256)(128)(2,1)}, u32[]{:S(2)}) copy-start(bf16[192]{0:T(256)(128)(2,1)} %param.32) | copy-start | bytes 1156
  129.9 109.9 %all-gather.13.cloned.1.call-start = ((), (), s32[]{:S(2)}) async-start(), calls=%async_computation.7 | async-start | bytes 3538944 | tf_op jit(solution)/shard_map/all_gather | solution.py:173
  130.7 165.7 %all-gather.11.cloned.1.call-start = ((), (), s32[]{:S(2)}) async-start(), calls=%async_computation.6 | async-start | bytes 6684672 | tf_op jit(solution)/shard_map/all_gather | solution.py:170
  198.0 1.0 copy-start.4
  238.6 86.7 %all-gather.17.cloned.1.call-start = ((), (), s32[]{:S(2)}) async-start(), calls=%async_computation.9 | async-start | bytes 3538944 | tf_op jit(solution)/shard_map/all_gather | solution.py:184
  239.2 115.5 %all-gather.15.cloned.1.call-start = ((), (), s32[]{:S(2)}) async-start(), calls=%async_computation.8 | async-start | bytes 3538944 | tf_op jit(solution)/shard_map/all_gather | solution.py:178
  239.8 209.5 %reduce-scatter.2.cloned.1.call-start = ((), (), s32[]{:S(2)}) async-start(), calls=%async_computation.10 | async-start | bytes 6684672 | tf_op jit(solution)/shard_map/reduce_scatter | solution.py:187
  367.5 1.0 copy-start.2
  367.5 2.7 copy-start.5
Sparse Core Ops, SparseCore 0:
  24.8 25.2 all-gather.8
  130.1 63.0 all-gather.6
  194.8 27.2 all-gather.12
  238.7 57.6 all-gather.10
  298.0 27.2 all-gather.16
  326.8 27.8 all-gather.14
  367.6 81.6 reduce-scatter.1
where the time goes:
time: 459 us; the launch traced here: 458 us
  waiting for transfers between devices  259 us (56%)
  local copies, waits for them, and re-layouts  51.6 us (11%)
  matrix products  48 us (10%)
  blocking collectives  38.4 us (8%)
  other arithmetic  25 us (5%)
  starting transfers between devices  20.3 us (4%)
  between operations  15.9 us (3%)
    reduce_scatter x1, waiting for transfers between devices, body(): lax.psum_scatter(partial_terms.astype(jnp.bfloat16), 'col', scatter_dimen...  77.5 us
    all_gather x1, waiting for transfers between devices, body(): lax.all_gather(attended, 'col', axis=0, tiled=True)  60.7 us
    all_gather x1, waiting for transfers between devices, body(): gathered = lax.all_gather(normed, 'col', axis=1, tiled=True)  56.6 us
    psum x1, blocking collectives, body(): row_totals = lax.psum(local_sums, 'col')  38.4 us
    all_gather x1, waiting for transfers between devices, body(): lax.all_gather(up_weight, 'row', axis=0, tiled=True)  29.4 us
    unnamed x21, local copies, waits for them, and re-layouts  29 us
    all_gather x1, waiting for transfers between devices, body(): lax.all_gather(down_weight, 'row', axis=1, tiled=True)  22.3 us
    dot_general x1, matrix products, body(): jnp.dot(hidden, lax.all_gather(down_weight, 'row', axis=1, tiled=True), p...  12.8 us
  transfers between devices with their start and end apart: 10, of which 6 were waited for; matrix products, arithmetic and copies ran while one was open for 22% of the time, Pallas kernels for 0%

commit v1 on v0

--- a/solution.py
+++ b/solution.py
@@ -7,6 +7,28 @@
 D = 3072
 HEADS = 32
 HEAD_DIM = 96
+
+
+def joined_along(tiles, dim):
+    lengths = list(tiles.shape[1:])
+    lengths[dim] *= tiles.shape[0]
+    return jnp.moveaxis(tiles, 0, dim).reshape(lengths)
+
+
+def ring_gather(x, axis, dim):
+    size = lax.axis_size(axis)
+    pairs = [(i, (i + 1) % size) for i in range(size)]
+    back = [(b, a) for a, b in pairs]
+    lower, upper = ([], [])
+    for step in range(size - 1):
+        if step % 2 == 0:
+            lower.append(lax.ppermute(lower[-1] if lower else x, axis, pairs))
+        else:
+            upper.append(lax.ppermute(upper[-1] if upper else x, axis, back))
+    tiles = jnp.stack([*lower[::-1], x, *upper])
+    shift = lax.axis_index(axis) - len(lower)
+    tiles = tiles[(jnp.arange(size) - shift) % size]
+    return joined_along(tiles, dim)
 
 
 def ancestry(parent_row):
@@ -174,9 +196,7 @@
         preferred_element_type=jnp.float32,
     )
     up_next = jnp.dot(
-        gathered,
-        lax.all_gather(up_weight, "row", axis=0, tiled=True),
-        preferred_element_type=jnp.float32,
+        gathered, ring_gather(up_weight, "row", 0), preferred_element_type=jnp.float32
     )
     hidden = (jax.nn.silu(gate_next) * up_next).astype(jnp.bfloat16)
     partial_terms = jnp.dot(

time: 459 us -> 430 us (0.937)
  waiting for transfers between devices: 259 us -> 209 us
  local copies, waits for them, and re-layouts: 51.6 us -> 63.2 us
  starting transfers between devices: 20.3 us -> 29.3 us
    all_gather x1, waiting for transfers between devices: 56.6 us -> 11.8 us  [body(): gathered = lax.all_gather(normed, 'col', axis=1, tiled=True)]
    all_gather x1 -> x0, waiting for transfers between devices: 29.4 us -> none  [body(): lax.all_gather(up_weight, 'row', axis=0, tiled=True)]
    ppermute x0 -> x7, waiting for transfers between devices: none -> 24.7 us  [the longest x4 24.7 us: ring_gather(): lower.append(lax.ppermute(lower[-1] if lower else x, axis, pairs))]
    ppermute x0 -> x7, starting transfers between devices: none -> 9.03 us  [the longest x3 9 us: ring_gather(): upper.append(lax.ppermute(upper[-1] if upper else x, axis, back))]
    unnamed x21 -> x30, local copies, waits for them, and re-layouts: 29 us -> 35.5 us
  transfers between devices with their start and end apart: 10 -> 16, of which waited for: 6 -> 9; matrix products, arithmetic and copies ran while one was open for 22% -> 26% of each run, Pallas kernels for 0% -> 0%
where the time goes in v1:
time: 430 us; the launch traced here: 429 us
  waiting for transfers between devices  209 us (49%)
  local copies, waits for them, and re-layouts  63.2 us (15%)
  matrix products  48 us (11%)
  blocking collectives  38.4 us (9%)
  starting transfers between devices  29.3 us (7%)
  other arithmetic  25 us (6%)
  between operations  15.9 us (4%)
    reduce_scatter x1, waiting for transfers between devices, body(): lax.psum_scatter(partial_terms.astype(jnp.bfloat16), 'col', scatter_dimen...  77.7 us
    all_gather x1, waiting for transfers between devices, body(): lax.all_gather(attended, 'col', axis=0, tiled=True)  60.7 us
    psum x1, blocking collectives, body(): row_totals = lax.psum(local_sums, 'col')  38.4 us
    unnamed x30, local copies, waits for them, and re-layouts  35.5 us
    ppermute x4, waiting for transfers between devices, ring_gather(): lower.append(lax.ppermute(lower[-1] if lower else x, axis, pairs))  24.7 us
    all_gather x1, waiting for transfers between devices, body(): lax.all_gather(down_weight, 'row', axis=1, tiled=True)  22.3 us
    dot_general x1, matrix products, body(): jnp.dot(hidden, lax.all_gather(down_weight, 'row', axis=1, tiled=True), p...  12.8 us
    all_gather x1, waiting for transfers between devices, body(): gathered = lax.all_gather(normed, 'col', axis=1, tiled=True)  11.8 us
  transfers between devices with their start and end apart: 16, of which 9 were waited for; matrix products, arithmetic and copies ran while one was open for 26% of the time, Pallas kernels for 0%

profile of v1, /device:TPU:0, one launch (start us, length us, event | category | flops | bytes accessed | tf_op | source)
XLA Modules:
  0.0 428.7 jit_solution(16160741608175756156)
XLA Ops:
  14.3 8.0 %all-to-all-start.1 = ((bf16[16,64,192]{2,1,0:T(8,128)(2,1)}), bf16[16,64,192]{2,1,0:T(8,128)(2,1)S(1)}, u32[]{:S(2)}, u32[]{:S(2)}) async-start(bf16[16,64,192]{2,1,0:T(8,128)(2,1)} %get-tuple-element.212), calls=%async_computation.1 | async-start | bytes 1048576 | tf_op jit(solution)/shard_map/all_to_all | solution.py:161
  25.6 12.7 %copy.22 = bf16[1,1536,3072]{1,2,0:T(8,128)(2,1)} copy(bf16[1,1536,3072]{2,1,0:T(8,128)(2,1)} %param.25) | data formatting | bytes 18874368 | tf_op args[5]
  38.3 12.6 %copy.27 = bf16[1,1536,3072]{1,2,0:T(8,128)(2,1)} copy(bf16[1,1536,3072]{2,1,0:T(8,128)(2,1)} %param.26) | data formatting | bytes 18874368 | tf_op args[6]
  51.1 7.4 %all-to-all-start = ((bf16[16,64,192]{2,1,0:T(8,128)(2,1)}), bf16[16,64,192]{2,1,0:T(8,128)(2,1)}, u32[]{:S(2)}, u32[]{:S(2)}) async-start(bf16[16,64,192]{2,1,0:T(8,128)(2,1)} %get-tuple-element.213), calls=%async_computation | async-start | bytes 1048576 | tf_op jit(solution)/shard_map/all_to_all | solution.py:160
  59.9 9.6 %all-to-all-done = bf16[16,64,192]{2,1,0:T(8,128)(2,1)} async-done(((bf16[16,64,192]{2,1,0:T(8,128)(2,1)}), bf16[16,64,192]{2,1,0:T(8,128)(2,1)}, u32[]{:S(2)}, u32[]{:S(2)}) %all-to-all-start) | async-done | bytes 393248 | tf_op jit(solution)/shard_map/all_to_all | solution.py:160
  69.5 4.2 all-to-all-start.2
  82.6 40.5 %while.18 = (s32[]{:T(128)}, f32[32,64]{1,0:T(8,128)S(1)}, f32[32,64]{1,0:T(8,128)S(1)}, f32[64,32,96]{2,0,1:T(8,128)}, s32[]{:T(128)}, /*index=5*/bf16[1536,307...) while((s32[]{:T(128)}, f32[32,64]{1,0:T(8,128)S(1)}, ...), condition=%wide.region_5.7_spmd.clone, body=%wide.region_2.6_spmd.clone.sunk | while | flops 414790656 | bytes 51906808 | solution.py:115
  89.4 3.4 fusion.86
  105.7 3.6 fusion.88
  116.1 3.4 fusion.86
  119.6 3.6 fusion.88
  132.4 60.7 %all-gather.6.cloned.1.call-done = bf16[1024,3072]{1,0:T(8,128)(2,1)} async-done(((bf16[64,3072]{1,0:T(8,128)(2,1)}), bf16[1024,3072]{1,0:T(8,128)(2,1)}) %all-gather.6.cloned.1.call-update) | async-done | bytes 6291472 | tf_op jit(solution)/shard_map/all_gather | solution.py:177
  193.1 4.9 %fusion.47 = f32[1024,192]{1,0:T(8,128)S(1)} fusion(bf16[1024,3072]{1,0:T(8,128)(2,1)} %all-gather.6.cloned.1.call-done, bf16[3072,192]{0,1:T(8,128)(2,1)} %all-gather.8.cloned.1.call-done), kind=kOutput, calls=%fused_computation.114 | convolution fusion | flops 1207959552 | bytes 8257536 | tf_op jit(solution)/shard_map/dot_general | solution.py:176
  199.2 38.4 %psum.7 = f32[1024]{0:T(1024)S(1)} all-reduce(f32[1024]{0:T(1024)S(1)} %fusion.27), channel_id=1, replica_groups=mesh['row'=8,'col'=16] {'col'}, use_global_device_ids=true, to_apply=%region_9.11 | all-reduce | flops 1024 | bytes 8192 | tf_op jit(solution)/shard_map/psum | solution.py:189
  239.2 8.4 %collective-permute-done = bf16[384,512]{1,0:T(8,128)(2,1)S(1)} collective-permute-done((bf16[384,512]{1,0:T(8,128)(2,1)S(1)}, bf16[384,512]{1,0:T(8,128)(2,1)S(1)}, u32[]{:S(2)}, u32[]{:S(2)}) %collective-permute-start) | collective-permute-done | bytes 393248 | tf_op jit(solution)/shard_map/ppermute | solution.py:25
  250.5 5.5 %collective-permute-done.1 = bf16[384,512]{1,0:T(8,128)(2,1)S(1)} collective-permute-done((bf16[384,512]{1,0:T(8,128)(2,1)S(1)}, bf16[384,512]{1,0:T(8,128)(2,1)S(1)}, u32[]{:S(2)}, u32[]{:S(2)}) %collective-permute-start.1) | collective-permute-done | bytes 393248 | tf_op jit(solution)/shard_map/ppermute | solution.py:25
  259.0 5.4 %collective-permute-done.2 = bf16[384,512]{1,0:T(8,128)(2,1)S(1)} collective-permute-done((bf16[384,512]{1,0:T(8,128)(2,1)S(1)}, bf16[384,512]{1,0:T(8,128)(2,1)S(1)}, u32[]{:S(2)}, u32[]{:S(2)}) %collective-permute-start.2) | collective-permute-done | bytes 393248 | tf_op jit(solution)/shard_map/ppermute | solution.py:25
  267.5 5.5 %collective-permute-done.3 = bf16[384,512]{1,0:T(8,128)(2,1)} collective-permute-done((bf16[384,512]{1,0:T(8,128)(2,1)S(1)}, bf16[384,512]{1,0:T(8,128)(2,1)}, u32[]{:S(2)}, u32[]{:S(2)}) %collective-permute-start.3) | collective-permute-done | bytes 393248 | tf_op jit(solution)/shard_map/ppermute | solution.py:25
  280.2 4.4 %gather_fusion.1 = bf16[8,384,512]{2,1,0:T(8,128)(2,1)} fusion(bf16[8,384,512]{2,1,0:T(8,128)(2,1)} %bitcast_dynamic-update-slice_fusion, s32[1024]{0:T(1024)S(1)} %pad_clamp_fusion), kind=kCustom, calls=%fused_computation.4 | custom fusion | bytes 6291488 | tf_op jit(solution)/shard_map/gather | solution.py:30
  284.6 11.8 %all-gather.10.cloned.1.call-done = bf16[1024,3072]{0,1:T(8,128)(2,1)} async-done(((bf16[1024,192]{0,1:T(8,128)(2,1)}), bf16[1024,3072]{0,1:T(8,128)(2,1)}) %all-gather.10.cloned.1.call-update) | async-done | bytes 6291472 | tf_op jit(solution)/shard_map/all_gather | solution.py:192
  296.3 6.5 %fusion.48 = f32[1024,512]{1,0:T(8,128)S(1)} fusion(bf16[1024,3072]{0,1:T(8,128)(2,1)} %all-gather.10.cloned.1.call-done, bf16[3072,512]{1,0:T(8,128)(2,1)} %all-gather.12.cloned.1.call-done), kind=kOutput, calls=%fused_computation.115 | convolution fusion | flops 3221225472 | bytes 11534336 | tf_op jit(solution)/shard_map/dot_general | solution.py:193
  302.8 22.3 %all-gather.14.cloned.1.call-done = bf16[512,3072]{1,0:T(8,128)(2,1)} async-done(((bf16[512,384]{1,0:T(8,128)(2,1)}), bf16[512,3072]{1,0:T(8,128)(2,1)}) %all-gather.14.cloned.1.call-update) | async-done | bytes 3145744 | tf_op jit(solution)/shard_map/all_gather | solution.py:204
  325.2 12.8 %convolution_convert_fusion = bf16[1024,3072]{0,1:T(8,128)(2,1)} fusion(bf16[512,3072]{1,0:T(8,128)(2,1)} %all-gather.14.cloned.1.call-done, f32[1024,512]{1,0:T(8,128)S(1)} %fusion.48, bf16[1024,3072]{0,1:T(8,128)(2,1)} %all-gather.10.cloned.1.call-done, bf16[3072,512]{1,0:T(8,128)(2,1)} %bitcast.128), kind=kOutput, calls=%fused_computation.29 | convolution fusion | flops 6448742400 | bytes 20971520 | tf_op jit(solution)/shard_map/dot_general | solution.py:202
  342.3 77.7 %reduce-scatter.2.cloned.1.call-done = bf16[1024,192]{0,1:T(8,128)(2,1)} async-done(((bf16[1024,3072]{0,1:T(8,128)(2,1)}), bf16[1024,192]{0,1:T(8,128)(2,1)}) %reduce-scatter.2.cloned.1.call-update) | async-done | bytes 393232 | tf_op jit(solution)/shard_map/reduce_scatter | solution.py:207
  (150 shorter events, 80.1 us)
Async XLA Ops:
  7.2 5.0 %copy-start.3 = (bf16[1024,192]{0,1:T(8,128)(2,1)S(1)}, bf16[1024,192]{0,1:T(8,128)(2,1)}, u32[]{:S(2)}) copy-start(bf16[1024,192]{0,1:T(8,128)(2,1)} %param.22) | copy-start | bytes 1179652
  12.2 10.9 %copy-start.7 = (s32[1,64]{1,0:T(1,128)S(1)}, s32[1,64]{1,0:T(1,128)}, u32[]{:S(2)}) copy-start(s32[1,64]{1,0:T(1,128)} %param.28) | copy-start | bytes 772
  14.3 36.8 %all-to-all-start.1 = ((bf16[16,64,192]{2,1,0:T(8,128)(2,1)}), bf16[16,64,192]{2,1,0:T(8,128)(2,1)S(1)}, u32[]{:S(2)}, u32[]{:S(2)}) async-start(bf16[16,64,192]{2,1,0:T(8,128)(2,1)} %get-tuple-element.212), calls=%async_computation.1 | async-start | bytes 1048576 | tf_op jit(solution)/shard_map/all_to_all | solution.py:161
  22.3 110.1 %all-gather.8.cloned.1.call-start = ((), (), s32[]{:S(2)}) async-start(), calls=%async_computation.5 | async-start | bytes 1327104 | tf_op jit(solution)/shard_map/all_gather | solution.py:175
  51.1 18.4 %all-to-all-start = ((bf16[16,64,192]{2,1,0:T(8,128)(2,1)}), bf16[16,64,192]{2,1,0:T(8,128)(2,1)}, u32[]{:S(2)}, u32[]{:S(2)}) async-start(bf16[16,64,192]{2,1,0:T(8,128)(2,1)} %get-tuple-element.213), calls=%async_computation | async-start | bytes 1048576 | tf_op jit(solution)/shard_map/all_to_all | solution.py:160
  69.5 53.7 %all-to-all-start.2 = ((bf16[16,64,192]{2,1,0:T(8,128)(2,1)}), bf16[16,64,192]{2,1,0:T(8,128)(2,1)}, u32[]{:S(2)}, u32[]{:S(2)}) async-start(bf16[16,64,192]{2,1,0:T(8,128)(2,1)} %get-tuple-element.211), calls=%async_computation.2 | async-start | bytes 1048576 | tf_op jit(solution)/shard_map/all_to_all | solution.py:162
  73.7 119.3 %all-gather.6.cloned.1.call-start = ((), (), s32[]{:S(2)}) async-start(), calls=%async_computation.4 | async-start | bytes 6684672 | tf_op jit(solution)/shard_map/all_gather | solution.py:177
  89.4 3.4 copy-start
  102.3 3.4 copy-start
  123.1 3.6 copy-start.10
  126.8 4.1 copy-start.8
  126.8 5.5 %copy-start.9 = (bf16[192]{0:T(256)(128)(2,1)S(1)}, bf16[192]{0:T(256)(128)(2,1)}, u32[]{:S(2)}) copy-start(bf16[192]{0:T(256)(128)(2,1)} %param.32) | copy-start | bytes 1156
  129.9 154.7 %all-gather.12.cloned.1.call-start = ((), (), s32[]{:S(2)}) async-start(), calls=%async_computation.7 | async-start | bytes 3538944 | tf_op jit(solution)/shard_map/all_gather | solution.py:195
  130.6 165.7 %all-gather.10.cloned.1.call-start = ((), (), s32[]{:S(2)}) async-start(), calls=%async_computation.6 | async-start | bytes 6684672 | tf_op jit(solution)/shard_map/all_gather | solution.py:192
  198.6 40.6 %copy-start.4 = (bf16[384,512]{1,0:T(8,128)(2,1)S(1)}, bf16[384,512]{1,0:T(8,128)(2,1)}, u32[]{:S(2)}) copy-start(bf16[384,512]{1,0:T(8,128)(2,1)} %param.34) | copy-start | bytes 1179652
  238.5 86.7 %all-gather.14.cloned.1.call-start = ((), (), s32[]{:S(2)}) async-start(), calls=%async_computation.8 | async-start | bytes 3538944 | tf_op jit(solution)/shard_map/all_gather | solution.py:204
  239.1 180.9 %reduce-scatter.2.cloned.1.call-start = ((), (), s32[]{:S(2)}) async-start(), calls=%async_computation.9 | async-start | bytes 6684672 | tf_op jit(solution)/shard_map/reduce_scatter | solution.py:207
  239.2 8.4 %collective-permute-start = (bf16[384,512]{1,0:T(8,128)(2,1)S(1)}, bf16[384,512]{1,0:T(8,128)(2,1)S(1)}, u32[]{:S(2)}, u32[]{:S(2)}) collective-permute-start(bf16[384,512]{1,0:T(8,128)(2,1)S(1)} %copy-done.4), channel_id=1, source_target_pairs={{0,16},{16,32},{32,48},{48,64},{64,80},{80,96},{96,112},{112,0},{1... | collective-permute-start | bytes 1179656 | tf_op jit(solution)/shard_map/ppermute | solution.py:25
  247.6 8.4 %collective-permute-start.1 = (bf16[384,512]{1,0:T(8,128)(2,1)S(1)}, bf16[384,512]{1,0:T(8,128)(2,1)S(1)}, u32[]{:S(2)}, u32[]{:S(2)}) collective-permute-start(bf16[384,512]{1,0:T(8,128)(2,1)S(1)} %collective-permute-done), channel_id=1, source_target_pairs={{0,16},{16,32},{32,48},{48,64},{64,80},{80,96},{96,112},{112,0},{1... | collective-permute-start | bytes 1179656 | tf_op jit(solution)/shard_map/ppermute | solution.py:25
  247.6 8.4 %collective-permute-start.4 = (bf16[384,512]{1,0:T(8,128)(2,1)S(1)}, bf16[384,512]{1,0:T(8,128)(2,1)S(1)}, u32[]{:S(2)}, u32[]{:S(2)}) collective-permute-start(bf16[384,512]{1,0:T(8,128)(2,1)S(1)} %copy-done.4), channel_id=1, source_target_pairs={{16,0},{32,16},{48,32},{64,48},{80,64},{96,80},{112,96},{0,112},{1... | collective-permute-start | bytes 1179656 | tf_op jit(solution)/shard_map/ppermute | solution.py:27
  256.0 8.4 %collective-permute-start.2 = (bf16[384,512]{1,0:T(8,128)(2,1)S(1)}, bf16[384,512]{1,0:T(8,128)(2,1)S(1)}, u32[]{:S(2)}, u32[]{:S(2)}) collective-permute-start(bf16[384,512]{1,0:T(8,128)(2,1)S(1)} %collective-permute-done.1), channel_id=1, source_target_pairs={{0,16},{16,32},{32,48},{48,64},{64,80},{80,96},{96,112},{112,0},{1... | collective-permute-start | bytes 1179656 | tf_op jit(solution)/shard_map/ppermute | solution.py:25
  256.0 8.4 %collective-permute-start.5 = (bf16[384,512]{1,0:T(8,128)(2,1)S(1)}, bf16[384,512]{1,0:T(8,128)(2,1)S(1)}, u32[]{:S(2)}, u32[]{:S(2)}) collective-permute-start(bf16[384,512]{1,0:T(8,128)(2,1)S(1)} %collective-permute-done.4), channel_id=1, source_target_pairs={{16,0},{32,16},{48,32},{64,48},{80,64},{96,80},{112,96},{0,112},{1... | collective-permute-start | bytes 1179656 | tf_op jit(solution)/shard_map/ppermute | solution.py:27
  264.4 8.5 %collective-permute-start.3 = (bf16[384,512]{1,0:T(8,128)(2,1)S(1)}, bf16[384,512]{1,0:T(8,128)(2,1)}, u32[]{:S(2)}, u32[]{:S(2)}) collective-permute-start(bf16[384,512]{1,0:T(8,128)(2,1)S(1)} %collective-permute-done.2), channel_id=1, source_target_pairs={{0,16},{16,32},{32,48},{48,64},{64,80},{80,96},{96,112},{112,0},{1... | collective-permute-start | bytes 1179656 | tf_op jit(solution)/shard_map/ppermute | solution.py:25
  264.4 15.0 %collective-permute-start.6 = (bf16[384,512]{1,0:T(8,128)(2,1)S(1)}, bf16[384,512]{1,0:T(8,128)(2,1)S(1)}, u32[]{:S(2)}, u32[]{:S(2)}) collective-permute-start(bf16[384,512]{1,0:T(8,128)(2,1)S(1)} %collective-permute-done.5), channel_id=1, source_target_pairs={{16,0},{32,16},{48,32},{64,48},{80,64},{96,80},{112,96},{0,112},{1... | collective-permute-start | bytes 1179656 | tf_op jit(solution)/shard_map/ppermute | solution.py:27
  (7 other events, 18.1 us)
Sparse Core Ops, SparseCore 0:
  24.8 25.2 all-gather.7
  130.0 63.0 all-gather.5
  194.8 27.2 all-gather.11
  238.6 57.6 all-gather.9
  297.9 27.2 all-gather.13
  338.1 81.8 reduce-scatter.1
